TPU v7x, 512 devices: a whole 4x4x16 slice. The times are simulated.
512 devices in a mesh: stream: 32 (over z, x_hi), span: 16 (over y, x_lo, core).
Axes of the slice: x: 4 (x_hi: 2, x_lo: 2; x = x_hi * 2 + x_lo), y: 4, z: 16, core: 2. Of those that a mesh axis runs over, the one named last changes fastest.
Arguments:
- checkpoint: float32 [5, 192, 32, 2048], P(None, None, 'stream', 'span'), may hold values from -4.8 to 4.8
- adjoint: float32 [5, 192, 32, 2048], P(None, None, 'stream', 'span'), may hold values from -6 to 6
- line_inverse: bfloat16 [32, 3, 320, 320], P('stream'), may hold values from -0.3125 to 0.3125
- row_source: int32 [3072], replicated, may hold values from 0 to 3071, as said below
Outputs:
- adjoint_start: float32 [5, 192, 32, 2048], P(None, None, 'stream', 'span')
Inputs may be any that keep to these rules, and one draw needn't show every extreme that they name: `row_source`: every rotor outlet row is taken by exactly one stator inlet row, and each stator span tile takes exactly 12 rows from each rotor span tile.
All inputs are finite; a program needn't handle non-finite values.
Results may differ from a plain program's by a relative error of at most 0.0029.
Values sent between devices are 32-bit elements; how exact they have to be, the bound alone decides.
A program may use at most 64 MiB of HBM per device.

v0:
```python
import jax
import jax.numpy as jnp
from jax import lax
from jax.sharding import PartitionSpec as P

time_step = 0.5
ADVECTION = (1.0, 0.6, 0.8, 1.2, 0.7)
DISSIPATION = (0.3, 0.25, 0.35, 0.3, 0.4)
SPREADING = (0.4, 0.3, 0.5, 0.35, 0.45)


def with_halo(block, sides, width):
    for axis, dim in sides:
        count = lax.axis_size(axis)
        forward = [(i, i + 1) for i in range(count - 1)]
        forward.append((count - 1, 0))
        backward = [(target, source) for source, target in forward]
        low = lax.ppermute(
            lax.slice_in_dim(block, block.shape[dim] - width, None, axis=dim), axis, forward
        )
        high = lax.ppermute(lax.slice_in_dim(block, 0, width, axis=dim), axis, backward)
        block = jnp.concatenate([low, block, high], axis=dim)
    return block


def per_state(values):
    return jnp.array(values, jnp.float32).reshape(5, 1, 1, 1)


def plane_remap(lower_rim, upper_rim, row_source):
    span_count = lax.axis_size("span")
    position = lax.axis_index("span")
    line_points = lower_rim.shape[1]
    capacity = line_points // span_count
    src_dev = (row_source // line_points).reshape(span_count, line_points)
    src_row = (row_source % line_points).reshape(span_count, line_points)
    devices = jnp.arange(span_count, dtype=jnp.int32)
    slot_ids = jnp.arange(capacity, dtype=jnp.int32)
    point_ids = jnp.arange(line_points, dtype=jnp.int32)
    onehot = (src_dev[:, :, None] == devices[None, None, :]).astype(jnp.int32)
    arrival = jnp.sum((jnp.cumsum(onehot, axis=1) - onehot) * onehot, axis=2)
    pick_lower = (
        (src_dev == position)[:, :, None] & (arrival[:, :, None] == slot_ids[None, None, :])
    ).astype(jnp.int32)
    send_lower = jnp.sum(pick_lower * src_row[:, :, None], axis=1).reshape(span_count * capacity)
    own_dev = lax.dynamic_index_in_dim(src_dev, position, 0, keepdims=False)
    own_arrival = lax.dynamic_index_in_dim(arrival, position, 0, keepdims=False)
    pick_upper = (
        (own_dev[None, :] == devices[:, None])[:, :, None]
        & (own_arrival[None, :, None] == slot_ids[None, None, :])
    ).astype(jnp.int32)
    send_upper = jnp.sum(pick_upper * point_ids[None, :, None], axis=1).reshape(
        span_count * capacity
    )
    outgoing = (jnp.take(lower_rim, send_lower, axis=1), jnp.take(upper_rim, send_upper, axis=1))
    got_lower, got_upper = (
        lax.all_to_all(outgoing[0], "span", split_axis=1, concat_axis=1, tiled=True),
        lax.all_to_all(outgoing[1], "span", split_axis=1, concat_axis=1, tiled=True),
    )
    lower_mapped = jnp.take(got_lower, own_dev * capacity + own_arrival, axis=1)
    matches = (
        (src_dev == position)[:, :, None] & (src_row[:, :, None] == point_ids[None, None, :])
    ).astype(jnp.int32)
    where_from = devices[:, None] * capacity + arrival
    upper_pos = jnp.sum(matches * where_from[:, :, None], axis=(0, 1))
    upper_mapped = jnp.take(got_upper, upper_pos, axis=1)
    return (lower_mapped, upper_mapped)


def gather_rims(field, row_source):
    stream_count = lax.axis_size("stream")
    stream_place = lax.axis_index("stream")
    halfway = stream_count // 2
    padded = with_halo(field, (("stream", 2), ("span", 3)), 1)
    lower_rim = padded[:, :, 0, 1:-1]
    upper_rim = padded[:, :, -1, 1:-1]
    left_rim = padded[:, :, 1:-1, :-2]
    right_rim = padded[:, :, 1:-1, 2:]
    lower_rim = jnp.where(stream_place == 0, 0.0, lower_rim)
    upper_rim = jnp.where(stream_place == stream_count - 1, 0.0, upper_rim)
    lower_mapped, upper_mapped = plane_remap(lower_rim, upper_rim, row_source)
    lower_rim = jnp.where(stream_place == halfway, lower_mapped, lower_rim)
    upper_rim = jnp.where(stream_place == halfway - 1, upper_mapped, upper_rim)
    return (lower_rim, upper_rim, left_rim, right_rim)


def apply_operator(field, rims, coef_down, coef_up, center, lateral):
    lower_rim, upper_rim, left_rim, right_rim = rims
    upstream = jnp.concatenate([lower_rim[:, :, None], field[:, :, :-1]], axis=2)
    downstream = jnp.concatenate([field[:, :, 1:], upper_rim[:, :, None]], axis=2)
    lateral_sum = left_rim + right_rim - 2.0 * field
    return coef_down * downstream + coef_up * upstream + center * field + lateral * lateral_sum


def local(checkpoint, adjoint, line_inverse, row_source):
    advect = per_state(ADVECTION)
    dissip = per_state(DISSIPATION)
    lateral = per_state(SPREADING)
    toward_down = -0.5 * advect + dissip
    toward_up = 0.5 * advect + dissip
    center = -2.0 * dissip
    flux = jnp.tanh(checkpoint)
    flux_rims = gather_rims(flux, row_source)
    advanced = checkpoint + time_step * apply_operator(
        flux, flux_rims, toward_down, toward_up, center, lateral
    )
    tanh_adv = jnp.tanh(advanced)
    section_slope = 2.0 - tanh_adv * tanh_adv
    line_points = checkpoint.shape[1]
    stations = checkpoint.shape[2]
    span_cells = checkpoint.shape[3]
    blocks = line_inverse.shape[1]
    block_points = line_points // blocks
    rounded = adjoint.astype(jnp.bfloat16).reshape(5, blocks, block_points, stations, span_cells)
    inverse = line_inverse.reshape(stations, blocks, 5, block_points, 5, block_points)
    carried = jnp.einsum(
        "sbclem,cblsp->ebmsp", inverse, rounded, preferred_element_type=jnp.float32
    ).reshape(5, line_points, stations, span_cells)
    weighted = section_slope * carried
    weight_rims = gather_rims(weighted, row_source)
    tangent = 1.0 - flux * flux
    return weighted + time_step * tangent * apply_operator(
        weighted, weight_rims, toward_up, toward_down, center, lateral
    )


def solution(mesh):
    return jax.shard_map(
        local,
        mesh=mesh,
        in_specs=(
            P(None, None, "stream", "span"),
            P(None, None, "stream", "span"),
            P("stream", None, None, None),
            P(),
        ),
        out_specs=P(None, None, "stream", "span"),
        check_vma=False,
    )
```

profile of v0, /device:TPU:4, one launch (start us, length us, event | category | flops | bytes accessed | tf_op | source)
XLA Modules:
  0.0 159.7 jit_solution(2668991006154800796)
XLA Ops:
  0.0 1.9 %tanh_bitcast_fusion = (f32[5,192,1,128]{3,1,2,0:T(8,128)}, f32[5,192,1,128]{3,1,0,2:T(8,128)S(1)}) fusion(f32[5,192,1,128]{3,1,0,2:T(8,128)} %bitcast.151), kind=kLoop, calls=%fused_computation.113 | loop fusion | bytes 1474560 | tf_op jit(solution)/shard_map/tanh | solution.py:102
  1.9 7.8 %collective-permute-start = (f32[5,192,1,128]{3,1,2,0:T(8,128)}, f32[5,192,1,128]{3,1,2,0:T(8,128)S(1)}, u32[]{:S(2)}, u32[]{:S(2)}) collective-permute-start(f32[5,192,1,128]{3,1,2,0:T(8,128)} %get-tuple-element.12), channel_id=1, source_target_pairs={{16,0},{32,16},{48,32},{64,48},{80,64},{96,80},{112,96},{128,112},... | collective-permute-start | bytes 1474568 | tf_op jit(solution)/shard_map/ppermute | solution.py:21
  9.7 1.9 %collective-permute-start.1 = (f32[5,192,1,128]{3,1,2,0:T(8,128)}, f32[5,192,1,128]{3,1,2,0:T(8,128)S(1)}, u32[]{:S(2)}, u32[]{:S(2)}) collective-permute-start(f32[5,192,1,128]{3,1,2,0:T(8,128)} %get-tuple-element.12), channel_id=1, source_target_pairs={{0,16},{16,32},{32,48},{48,64},{64,80},{80,96},{96,112},{112,128},... | collective-permute-start | bytes 1474568 | tf_op jit(solution)/shard_map/ppermute | solution.py:18
  11.9 9.1 %reduce-window.6 = s32[16,16,2,128]{3,1,2,0:T(8,128)S(1)} reduce-window(s32[16,16,2,128]{3,1,2,0:T(8,128)S(1)} %copy_bitcast_fusion, s32[]{:T(128)} %constant.84.clone.1), window={size=1x1x1x128 pad=0_0x0_0x0_0x127_0}, to_apply=%region_0.1 | reduce-window | flops 8323072 | bytes 524292 | tf_op jit(solution)/shard_map/reduce-window
  22.8 2.5 %reshape.161 = bf16[3,5,64,5,64]{4,3,2,1,0:T(8,128)(2,1)S(1)} reshape(bf16[1,3,320,320]{3,2,1,0:T(8,128)(2,1)} %param.11) | data formatting | bytes 1228800 | tf_op jit(solution)/shard_map/reshape.24
  25.3 1.4 convert_element_type.6
  26.6 0.7 copy.179
  27.5 1.7 %select_reduce_fusion = s32[192]{0:T(256)S(1)} fusion(s32[16,192]{1,0:T(8,128)S(1)} %broadcast_add_fusion, s32[16,192]{1,0:T(8,128)S(1)} %eq.175, pred[16,192]{1,0:T(8,128)(4,1)S(1)} %broadcast_compare_fusion), kind=kLoop, calls=%fused_computation.8 | loop fusion | flops 2359104 | bytes 28416 | tf_op jit(solution)/shard_map/reduce_sum | solution.py:65
  29.2 2.2 %fusion.3 = f32[5,3,64,1,128]{4,2,0,1,3:T(8,128)} fusion(bf16[3,5,64,5,64]{4,3,2,1,0:T(8,128)(2,1)S(1)} %reshape.161, bf16[5,3,64,128,1]{3,2,1,0,4:T(8,128)(2,1)} %bitcast.159), kind=kOutput, calls=%fused_computation.15 | convolution fusion | flops 78643200 | bytes 1351680 | tf_op jit(solution)/shard_map/sbclem,cblsp->ebmsp/dot_general | solution.py:116
  31.8 0.9 gather_fusion.2
  32.7 1.2 select_bitcast_fusion.2
  33.9 3.7 %all-to-all-start.1 = ((f32[5,192,128]{2,0,1:T(8,128)}), f32[5,192,128]{2,0,1:T(8,128)S(1)}, u32[]{:S(2)}, u32[]{:S(2)}) async-start(f32[5,192,128]{2,0,1:T(8,128)} %select_bitcast_fusion.2), calls=%async_computation.1 | async-start | bytes 1572864 | tf_op jit(solution)/shard_map/all_to_all | solution.py:57
  38.0 1.8 %gather_fusion = f32[192,5,128]{2,1,0:T(8,128)} fusion(f32[5,192,128]{2,0,1:T(8,128)S(1)} %copy.140, s32[1024]{0:T(1024)S(1)} %pad_clamp_fusion.3), kind=kCustom, calls=%fused_computation.clone | custom fusion | bytes 983808 | tf_op jit(solution)/shard_map/jit(_take)/gather | solution.py:55
  39.8 2.3 %select_bitcast_fusion.3 = f32[5,192,128]{2,0,1:T(8,128)} fusion(f32[192,5,128]{2,1,0:T(8,128)} %gather_fusion, pred[192]{0:T(512)(128)(4,1)S(1)} %compare_and_fusion.3), kind=kLoop, calls=%fused_computation.19 | loop fusion | flops 122880 | bytes 983232 | tf_op jit(solution)/shard_map/jit(_take)/select_n | solution.py:55
  42.1 9.3 %all-to-all-done.1 = f32[5,192,128]{2,0,1:T(8,128)S(1)} async-done(((f32[5,192,128]{2,0,1:T(8,128)}), f32[5,192,128]{2,0,1:T(8,128)S(1)}, u32[]{:S(2)}, u32[]{:S(2)}) %all-to-all-start.1) | async-done | bytes 491552 | tf_op jit(solution)/shard_map/all_to_all | solution.py:57
  51.4 4.3 %all-to-all-start = ((f32[5,192,128]{2,0,1:T(8,128)}), f32[5,192,128]{2,0,1:T(8,128)}, u32[]{:S(2)}, u32[]{:S(2)}) async-start(f32[5,192,128]{2,0,1:T(8,128)} %select_bitcast_fusion.3), calls=%async_computation | async-start | bytes 1572864 | tf_op jit(solution)/shard_map/all_to_all | solution.py:58
  55.8 0.5 fusion.39
  56.3 0.6 copy.151
  56.9 5.6 %collective-permute-start.3 = (f32[5,192,3,1]{1,3,2,0:T(1,128)S(1)}, f32[5,192,3,1]{1,3,2,0:T(1,128)S(1)}, u32[]{:S(2)}, u32[]{:S(2)}) collective-permute-start(f32[5,192,3,1]{1,3,2,0:T(1,128)S(1)} %copy.151), channel_id=1, source_target_pairs={{1,0},{2,1},{3,2},{4,3},{5,4},{6,5},{7,6},{8,7},{9,8},{10,9},{11,1... | collective-permute-start | bytes 34568 | tf_op jit(solution)/shard_map/ppermute | solution.py:21
  62.5 0.6 copy.149
  63.1 1.9 %collective-permute-start.2 = (f32[5,192,3,1]{1,3,2,0:T(1,128)S(1)}, f32[5,192,3,1]{1,3,2,0:T(1,128)S(1)}, u32[]{:S(2)}, u32[]{:S(2)}) collective-permute-start(f32[5,192,3,1]{1,3,2,0:T(1,128)S(1)} %copy.149), channel_id=1, source_target_pairs={{0,1},{1,2},{2,3},{3,4},{4,5},{5,6},{6,7},{7,8},{8,9},{9,10},{10,1... | collective-permute-start | bytes 34568 | tf_op jit(solution)/shard_map/ppermute | solution.py:18
  65.1 0.8 copy.158
  65.9 0.5 copy.152
  66.5 3.8 %collective-permute-done.2 = f32[5,192,3,1]{1,3,2,0:T(1,128)S(1)} collective-permute-done((f32[5,192,3,1]{1,3,2,0:T(1,128)S(1)}, f32[5,192,3,1]{1,3,2,0:T(1,128)S(1)}, u32[]{:S(2)}, u32[]{:S(2)}) %collective-permute-start.2) | collective-permute-done | bytes 11552 | tf_op jit(solution)/shard_map/ppermute | solution.py:18
  70.8 2.7 %gather_fusion.3 = f32[192,5,128]{2,1,0:T(8,128)} fusion(f32[5,192,128]{2,0,1:T(8,128)} %copy-done.6, s32[1024]{0:T(1024)S(1)} %pad_clamp_fusion), kind=kCustom, calls=%fused_computation.3.clone | custom fusion | bytes 983808 | tf_op jit(solution)/shard_map/jit(_take)/gather | solution.py:60
  73.5 2.7 %gather_fusion.1 = f32[192,5,128]{2,1,0:T(8,128)} fusion(f32[5,192,128]{2,0,1:T(8,128)} %all-to-all-done, s32[1024]{0:T(1024)S(1)} %pad_clamp_fusion.2), kind=kCustom, calls=%fused_computation.1.clone | custom fusion | bytes 983808 | tf_op jit(solution)/shard_map/jit(_take)/gather | solution.py:66
  76.3 3.9 %fusion.7 = f32[5,192,1,128]{3,1,2,0:T(8,128)} fusion(f32[5,192,1,128]{3,1,2,0:T(8,128)} %bitcast.158, f32[5,192,1,128]{3,1,0,2:T(8,128)S(1)} %bitcast.152, f32[5,192,1,128]{3,1,0,2:T(8,128)} %copy-done.1, f32[5,192,3,1]{3,1,0,2:T(8,128)S(1)} %copy.152, f32[5,192,1,128]{3,1,0,2:T(8,128)} %bitcast.155, f32[5,192,1,128]{3,1,0,2:T(8,128)} %bitcast.157, ...), kind=kLoop, calls=%fused_computation.23 | loop fusion | flops 3317760 | bytes 3955668 | tf_op jit(solution)/shard_map/mul | solution.py:119
  80.2 3.2 %collective-permute-start.5 = (f32[5,192,1,128]{3,1,2,0:T(8,128)}, f32[5,192,1,128]{3,1,2,0:T(8,128)S(1)}, u32[]{:S(2)}, u32[]{:S(2)}) collective-permute-start(f32[5,192,1,128]{3,1,2,0:T(8,128)} %fusion.7), channel_id=1, source_target_pairs={{0,16},{16,32},{32,48},{48,64},{64,80},{80,96},{96,112},{112,128},... | collective-permute-start | bytes 1474568 | tf_op jit(solution)/shard_map/ppermute | solution.py:18
  83.4 8.1 %collective-permute-start.4 = (f32[5,192,1,128]{3,1,2,0:T(8,128)}, f32[5,192,1,128]{3,1,2,0:T(8,128)S(1)}, u32[]{:S(2)}, u32[]{:S(2)}) collective-permute-start(f32[5,192,1,128]{3,1,2,0:T(8,128)} %fusion.7), channel_id=1, source_target_pairs={{16,0},{32,16},{48,32},{64,48},{80,64},{96,80},{112,96},{128,112},... | collective-permute-start | bytes 1474568 | tf_op jit(solution)/shard_map/ppermute | solution.py:21
  91.5 17.4 %collective-permute-done.5 = f32[5,192,1,128]{3,1,2,0:T(8,128)S(1)} collective-permute-done((f32[5,192,1,128]{3,1,2,0:T(8,128)}, f32[5,192,1,128]{3,1,2,0:T(8,128)S(1)}, u32[]{:S(2)}, u32[]{:S(2)}) %collective-permute-start.5) | collective-permute-done | bytes 491552 | tf_op jit(solution)/shard_map/ppermute | solution.py:18
  109.2 0.9 gather_fusion.6
  110.1 1.2 select_bitcast_fusion
  111.3 5.0 %all-to-all-start.3 = ((f32[5,192,128]{2,0,1:T(8,128)}), f32[5,192,128]{2,0,1:T(8,128)S(1)}, u32[]{:S(2)}, u32[]{:S(2)}) async-start(f32[5,192,128]{2,0,1:T(8,128)} %select_bitcast_fusion), calls=%async_computation.3 | async-start | bytes 1572864 | tf_op jit(solution)/shard_map/all_to_all | solution.py:57
  116.3 1.2 copy.162
  117.6 1.8 %gather_fusion.4 = f32[192,5,128]{2,1,0:T(8,128)S(1)} fusion(f32[5,192,128]{2,0,1:T(8,128)} %copy.162, s32[1024]{0:T(1024)S(1)} %pad_clamp_fusion.3), kind=kCustom, calls=%fused_computation.4.clone | custom fusion | bytes 983808 | tf_op jit(solution)/shard_map/jit(_take)/gather | solution.py:55
  119.4 1.2 select_bitcast_fusion.1
  120.6 9.4 %all-to-all-done.3 = f32[5,192,128]{2,0,1:T(8,128)S(1)} async-done(((f32[5,192,128]{2,0,1:T(8,128)}), f32[5,192,128]{2,0,1:T(8,128)S(1)}, u32[]{:S(2)}, u32[]{:S(2)}) %all-to-all-start.3) | async-done | bytes 491552 | tf_op jit(solution)/shard_map/all_to_all | solution.py:57
  130.0 4.5 %all-to-all-start.2 = ((f32[5,192,128]{2,0,1:T(8,128)}), f32[5,192,128]{2,0,1:T(8,128)}, u32[]{:S(2)}, u32[]{:S(2)}) async-start(f32[5,192,128]{2,0,1:T(8,128)} %select_bitcast_fusion.1), calls=%async_computation.2 | async-start | bytes 1572864 | tf_op jit(solution)/shard_map/all_to_all | solution.py:58
  134.5 1.1 pad_maximum_fusion.1
  135.7 0.5 fusion.38
  136.2 0.6 copy.170
  136.8 5.4 %collective-permute-start.7 = (f32[5,192,3,1]{1,3,2,0:T(1,128)S(1)}, f32[5,192,3,1]{1,3,2,0:T(1,128)S(1)}, u32[]{:S(2)}, u32[]{:S(2)}) collective-permute-start(f32[5,192,3,1]{1,3,2,0:T(1,128)S(1)} %copy.170), channel_id=1, source_target_pairs={{1,0},{2,1},{3,2},{4,3},{5,4},{6,5},{7,6},{8,7},{9,8},{10,9},{11,1... | collective-permute-start | bytes 34568 | tf_op jit(solution)/shard_map/ppermute | solution.py:21
  142.2 0.6 copy.168
  142.8 1.9 %collective-permute-start.6 = (f32[5,192,3,1]{1,3,2,0:T(1,128)S(1)}, f32[5,192,3,1]{1,3,2,0:T(1,128)S(1)}, u32[]{:S(2)}, u32[]{:S(2)}) collective-permute-start(f32[5,192,3,1]{1,3,2,0:T(1,128)S(1)} %copy.168), channel_id=1, source_target_pairs={{0,1},{1,2},{2,3},{3,4},{4,5},{5,6},{6,7},{7,8},{8,9},{9,10},{10,1... | collective-permute-start | bytes 34568 | tf_op jit(solution)/shard_map/ppermute | solution.py:18
  145.2 4.7 %collective-permute-done.6 = f32[5,192,3,1]{1,3,2,0:T(1,128)S(1)} collective-permute-done((f32[5,192,3,1]{1,3,2,0:T(1,128)S(1)}, f32[5,192,3,1]{1,3,2,0:T(1,128)S(1)}, u32[]{:S(2)}, u32[]{:S(2)}) %collective-permute-start.6) | collective-permute-done | bytes 11552 | tf_op jit(solution)/shard_map/ppermute | solution.py:18
  150.4 2.7 %gather_fusion.7 = f32[192,5,128]{2,1,0:T(8,128)} fusion(f32[5,192,128]{2,0,1:T(8,128)} %copy-done.7, s32[1024]{0:T(1024)S(1)} %pad_clamp_fusion), kind=kCustom, calls=%fused_computation.7.clone | custom fusion | bytes 983808 | tf_op jit(solution)/shard_map/jit(_take)/gather | solution.py:60
  153.2 2.7 %gather_fusion.5 = f32[192,5,128]{2,1,0:T(8,128)} fusion(f32[5,192,128]{2,0,1:T(8,128)} %all-to-all-done.2, s32[1024]{0:T(1024)S(1)} %pad_clamp_fusion.2), kind=kCustom, calls=%fused_computation.5.clone | custom fusion | bytes 983808 | tf_op jit(solution)/shard_map/jit(_take)/gather | solution.py:66
  155.9 3.7 %fusion.20 = f32[5,192,1,128]{3,1,2,0:T(8,128)} fusion(f32[5,192,1,128]{3,1,2,0:T(8,128)} %fusion.7, f32[5,192,3,1]{3,1,2,0:T(8,128)S(1)} %copy.171, f32[5,192,1,128]{3,1,2,0:T(8,128)} %copy-done.5, f32[5,192,1,128]{3,1,2,0:T(8,128)} %copy-done.4, f32[5,192,3,1]{3,1,2,0:T(8,128)S(1)} %copy.169, f32[192,5,128]{2,1,0:T(8,128)} %gather_fusion.7, ...), kind=kLoop, calls=%fused_computation.37 | loop fusion | flops 3317760 | bytes 3464148 | tf_op jit(solution)/shard_map/add | solution.py:122
  (81 shorter events, 4.7 us)
Async XLA Ops:
  0.0 11.6 %copy-start.9 = (s32[3072]{0:T(1024)S(1)}, s32[3072]{0:T(1024)}, u32[]{:S(2)}) copy-start(s32[3072]{0:T(1024)} %param.12) | copy-start | bytes 36868
  1.9 53.7 %copy-start.1 = (f32[5,192,1,128]{3,1,0,2:T(8,128)}, f32[5,192,1,128]{3,1,0,2:T(8,128)S(1)}, u32[]{:S(2)}) copy-start(f32[5,192,1,128]{3,1,0,2:T(8,128)S(1)} %get-tuple-element.13) | copy-start | bytes 1474564
  1.9 35.7 %collective-permute-start = (f32[5,192,1,128]{3,1,2,0:T(8,128)}, f32[5,192,1,128]{3,1,2,0:T(8,128)S(1)}, u32[]{:S(2)}, u32[]{:S(2)}) collective-permute-start(f32[5,192,1,128]{3,1,2,0:T(8,128)} %get-tuple-element.12), channel_id=1, source_target_pairs={{16,0},{32,16},{48,32},{64,48},{80,64},{96,80},{112,96},{128,112},... | collective-permute-start | bytes 1474568 | tf_op jit(solution)/shard_map/ppermute | solution.py:21
  9.7 21.7 %collective-permute-start.1 = (f32[5,192,1,128]{3,1,2,0:T(8,128)}, f32[5,192,1,128]{3,1,2,0:T(8,128)S(1)}, u32[]{:S(2)}, u32[]{:S(2)}) collective-permute-start(f32[5,192,1,128]{3,1,2,0:T(8,128)} %get-tuple-element.12), channel_id=1, source_target_pairs={{0,16},{16,32},{32,48},{48,64},{64,80},{80,96},{96,112},{112,128},... | collective-permute-start | bytes 1474568 | tf_op jit(solution)/shard_map/ppermute | solution.py:18
  31.4 24.2 %copy-start.3 = (f32[5,192,1,128]{3,1,2,0:T(8,128)}, f32[5,192,1,128]{3,1,2,0:T(8,128)S(1)}, u32[]{:S(2)}) copy-start(f32[5,192,1,128]{3,1,2,0:T(8,128)S(1)} %collective-permute-done.1) | copy-start | bytes 1474564
  33.9 17.5 %all-to-all-start.1 = ((f32[5,192,128]{2,0,1:T(8,128)}), f32[5,192,128]{2,0,1:T(8,128)S(1)}, u32[]{:S(2)}, u32[]{:S(2)}) async-start(f32[5,192,128]{2,0,1:T(8,128)} %select_bitcast_fusion.2), calls=%async_computation.1 | async-start | bytes 1572864 | tf_op jit(solution)/shard_map/all_to_all | solution.py:57
  37.6 18.1 %copy-start.2 = (f32[5,192,1,128]{3,1,2,0:T(8,128)}, f32[5,192,1,128]{3,1,2,0:T(8,128)S(1)}, u32[]{:S(2)}) copy-start(f32[5,192,1,128]{3,1,2,0:T(8,128)S(1)} %collective-permute-done) | copy-start | bytes 1474564
  51.4 4.3 %copy-start.6 = (f32[5,192,128]{2,0,1:T(8,128)}, f32[5,192,128]{2,0,1:T(8,128)S(1)}, u32[]{:S(2)}) copy-start(f32[5,192,128]{2,0,1:T(8,128)S(1)} %all-to-all-done.1) | copy-start | bytes 1474564
  51.4 22.1 %all-to-all-start = ((f32[5,192,128]{2,0,1:T(8,128)}), f32[5,192,128]{2,0,1:T(8,128)}, u32[]{:S(2)}, u32[]{:S(2)}) async-start(f32[5,192,128]{2,0,1:T(8,128)} %select_bitcast_fusion.3), calls=%async_computation | async-start | bytes 1572864 | tf_op jit(solution)/shard_map/all_to_all | solution.py:58
  56.3 8.7 %copy-start.8 = (f32[5,3,64,1,128]{4,2,0,1,3:T(8,128)S(1)}, f32[5,3,64,1,128]{4,2,0,1,3:T(8,128)}, u32[]{:S(2)}) copy-start(f32[5,3,64,1,128]{4,2,0,1,3:T(8,128)} %fusion.3) | copy-start | bytes 1474564
  56.9 9.0 %collective-permute-start.3 = (f32[5,192,3,1]{1,3,2,0:T(1,128)S(1)}, f32[5,192,3,1]{1,3,2,0:T(1,128)S(1)}, u32[]{:S(2)}, u32[]{:S(2)}) collective-permute-start(f32[5,192,3,1]{1,3,2,0:T(1,128)S(1)} %copy.151), channel_id=1, source_target_pairs={{1,0},{2,1},{3,2},{4,3},{5,4},{6,5},{7,6},{8,7},{9,8},{10,9},{11,1... | collective-permute-start | bytes 34568 | tf_op jit(solution)/shard_map/ppermute | solution.py:21
  63.1 7.2 %collective-permute-start.2 = (f32[5,192,3,1]{1,3,2,0:T(1,128)S(1)}, f32[5,192,3,1]{1,3,2,0:T(1,128)S(1)}, u32[]{:S(2)}, u32[]{:S(2)}) collective-permute-start(f32[5,192,3,1]{1,3,2,0:T(1,128)S(1)} %copy.149), channel_id=1, source_target_pairs={{0,1},{1,2},{2,3},{3,4},{4,5},{5,6},{6,7},{7,8},{8,9},{9,10},{10,1... | collective-permute-start | bytes 34568 | tf_op jit(solution)/shard_map/ppermute | solution.py:18
  66.4 9.9 %copy-start = (f32[5,192,1,128]{3,2,1,0:T(1,128)S(1)}, f32[5,192,1,128]{3,2,1,0:T(1,128)}, u32[]{:S(2)}) copy-start(f32[5,192,1,128]{3,2,1,0:T(1,128)} %param.9) | copy-start | bytes 1474564
  66.4 9.8 %copy-start.10 = (f32[5]{0:T(128)S(1)}, f32[5]{0:T(128)}, u32[]{:S(2)}) copy-start(f32[5]{0:T(128)} %constant.95.clone) | copy-start | bytes 64
  66.4 9.8 %copy-start.11 = (f32[5]{0:T(128)S(1)}, f32[5]{0:T(128)}, u32[]{:S(2)}) copy-start(f32[5]{0:T(128)} %constant.105) | copy-start | bytes 64
  66.5 9.8 %copy-start.12 = (f32[5]{0:T(128)S(1)}, f32[5]{0:T(128)}, u32[]{:S(2)}) copy-start(f32[5]{0:T(128)} %constant.104) | copy-start | bytes 64
  66.5 9.8 %copy-start.13 = (f32[5]{0:T(128)S(1)}, f32[5]{0:T(128)}, u32[]{:S(2)}) copy-start(f32[5]{0:T(128)} %constant.102) | copy-start | bytes 64
  80.2 28.6 %collective-permute-start.5 = (f32[5,192,1,128]{3,1,2,0:T(8,128)}, f32[5,192,1,128]{3,1,2,0:T(8,128)S(1)}, u32[]{:S(2)}, u32[]{:S(2)}) collective-permute-start(f32[5,192,1,128]{3,1,2,0:T(8,128)} %fusion.7), channel_id=1, source_target_pairs={{0,16},{16,32},{32,48},{48,64},{64,80},{80,96},{96,112},{112,128},... | collective-permute-start | bytes 1474568 | tf_op jit(solution)/shard_map/ppermute | solution.py:18
  83.4 32.9 %collective-permute-start.4 = (f32[5,192,1,128]{3,1,2,0:T(8,128)}, f32[5,192,1,128]{3,1,2,0:T(8,128)S(1)}, u32[]{:S(2)}, u32[]{:S(2)}) collective-permute-start(f32[5,192,1,128]{3,1,2,0:T(8,128)} %fusion.7), channel_id=1, source_target_pairs={{16,0},{32,16},{48,32},{64,48},{80,64},{96,80},{112,96},{128,112},... | collective-permute-start | bytes 1474568 | tf_op jit(solution)/shard_map/ppermute | solution.py:21
  108.9 25.6 %copy-start.4 = (f32[5,192,1,128]{3,1,2,0:T(8,128)}, f32[5,192,1,128]{3,1,2,0:T(8,128)S(1)}, u32[]{:S(2)}) copy-start(f32[5,192,1,128]{3,1,2,0:T(8,128)S(1)} %collective-permute-done.5) | copy-start | bytes 1474564
  111.3 18.7 %all-to-all-start.3 = ((f32[5,192,128]{2,0,1:T(8,128)}), f32[5,192,128]{2,0,1:T(8,128)S(1)}, u32[]{:S(2)}, u32[]{:S(2)}) async-start(f32[5,192,128]{2,0,1:T(8,128)} %select_bitcast_fusion), calls=%async_computation.3 | async-start | bytes 1572864 | tf_op jit(solution)/shard_map/all_to_all | solution.py:57
  116.3 18.2 %copy-start.5 = (f32[5,192,1,128]{3,1,2,0:T(8,128)}, f32[5,192,1,128]{3,1,2,0:T(8,128)S(1)}, u32[]{:S(2)}) copy-start(f32[5,192,1,128]{3,1,2,0:T(8,128)S(1)} %collective-permute-done.4) | copy-start | bytes 1474564
  130.0 4.5 %copy-start.7 = (f32[5,192,128]{2,0,1:T(8,128)}, f32[5,192,128]{2,0,1:T(8,128)S(1)}, u32[]{:S(2)}) copy-start(f32[5,192,128]{2,0,1:T(8,128)S(1)} %all-to-all-done.3) | copy-start | bytes 1474564
  130.0 23.1 %all-to-all-start.2 = ((f32[5,192,128]{2,0,1:T(8,128)}), f32[5,192,128]{2,0,1:T(8,128)}, u32[]{:S(2)}, u32[]{:S(2)}) async-start(f32[5,192,128]{2,0,1:T(8,128)} %select_bitcast_fusion.1), calls=%async_computation.2 | async-start | bytes 1572864 | tf_op jit(solution)/shard_map/all_to_all | solution.py:58
  136.8 8.0 %collective-permute-start.7 = (f32[5,192,3,1]{1,3,2,0:T(1,128)S(1)}, f32[5,192,3,1]{1,3,2,0:T(1,128)S(1)}, u32[]{:S(2)}, u32[]{:S(2)}) collective-permute-start(f32[5,192,3,1]{1,3,2,0:T(1,128)S(1)} %copy.170), channel_id=1, source_target_pairs={{1,0},{2,1},{3,2},{4,3},{5,4},{6,5},{7,6},{8,7},{9,8},{10,9},{11,1... | collective-permute-start | bytes 34568 | tf_op jit(solution)/shard_map/ppermute | solution.py:21
  142.8 7.2 %collective-permute-start.6 = (f32[5,192,3,1]{1,3,2,0:T(1,128)S(1)}, f32[5,192,3,1]{1,3,2,0:T(1,128)S(1)}, u32[]{:S(2)}, u32[]{:S(2)}) collective-permute-start(f32[5,192,3,1]{1,3,2,0:T(1,128)S(1)} %copy.168), channel_id=1, source_target_pairs={{0,1},{1,2},{2,3},{3,4},{4,5},{5,6},{6,7},{7,8},{8,9},{9,10},{10,1... | collective-permute-start | bytes 34568 | tf_op jit(solution)/shard_map/ppermute | solution.py:18
where the time goes:
time: 161 us; the launch traced here: 160 us
  starting transfers between devices  53.3 us (33%)
  waiting for transfers between devices  44.7 us (28%)
  local copies, waits for them, and re-layouts  30.7 us (19%)
  other arithmetic  28.1 us (17%)
  matrix products  2.23 us (1%)
    ppermute x4, starting transfers between devices, with_halo(): lax.ppermute(lax.slice_in_dim(block, 0, width, axis=dim), axis, backward)  26.9 us
    ppermute x4, waiting for transfers between devices, with_halo(): lax.ppermute(lax.slice_in_dim(block, block.shape[dim] - width, None, axis...  25.9 us
    all_to_all x2, waiting for transfers between devices, plane_remap(): lax.all_to_all(outgoing[0], 'span', split_axis=1, concat_axis=1, tiled=True)  18.8 us
    another operation x4, other arithmetic  9.3 us
    ppermute x4, starting transfers between devices, with_halo(): lax.ppermute(lax.slice_in_dim(block, block.shape[dim] - width, None, axis...  8.91 us
    all_to_all x2, starting transfers between devices, plane_remap(): lax.all_to_all(outgoing[1], 'span', split_axis=1, concat_axis=1, tiled=True)  8.73 us
    all_to_all x2, starting transfers between devices, plane_remap(): lax.all_to_all(outgoing[0], 'span', split_axis=1, concat_axis=1, tiled=True)  8.72 us
    gather x2, local copies, waits for them, and re-layouts, plane_remap(): upper_mapped = jnp.take(got_upper, upper_pos, axis=1)  5.49 us
  transfers between devices with their start and end apart: 12, of which 5 were waited for; matrix products, arithmetic and copies ran while one was open for 29% of the time, Pallas kernels for 0%

commit v1 on v0

v1 whole, which is shorter than its diff:
```python
import jax
import jax.numpy as jnp
from jax import lax
from jax.experimental import pallas as pl
from jax.experimental.pallas import tpu as pltpu
from jax.sharding import PartitionSpec as P

time_step = 0.5
ADVECTION = (1.0, 0.6, 0.8, 1.2, 0.7)
DISSIPATION = (0.3, 0.25, 0.35, 0.3, 0.4)
SPREADING = (0.4, 0.3, 0.5, 0.35, 0.45)
MESH = pl.DeviceIdType.MESH
NC, NL, CP, NB, LB = 5, 192, 128, 3, 64
HALF = NL // 2
F32, BF16, I32 = jnp.float32, jnp.bfloat16, jnp.int32


def pick(values, index):
    out = jnp.float32(values[-1])
    for i in range(len(values) - 1):
        out = jnp.where(index == i, jnp.float32(values[i]), out)
    return out


def split(x):
    hi = x.astype(BF16)
    return hi, (x - hi.astype(F32)).astype(BF16)


def dot(a, b, dims):
    return lax.dot_general(a, b, (dims, ((), ())), preferred_element_type=F32)


def div_rows(x):
    return lax.shift_right_logical(x * 5462, 20)


def kernel(
    n_stream, n_span, ck_h, adj_h, li_h, rs_h, o_ref,
    cx, adj, li, rs, cb, fo, fld, hb, ob, eo, es, er, ys, yr, tm, tmt,
    l_sem, ck_s, ck_r, ca_s, ca_r, z_s, z_r, i_s, i_r, eo_s, eo_r, e_s, e_r, o_s, o_r, ready,
):
    s = lax.axis_index("stream")
    p = lax.axis_index("span")
    n_z = n_stream // 2
    zi = n_z // 2 - 1
    cap = NL // n_span
    pad = yr.shape[3]
    h = lax.rem(s, 2)
    z = s // 2
    slots = 3 - lax.rem(h + p, 2)
    other_slots = 5 - slots
    up_iface = z == zi
    down_iface = z == zi + 1
    iface = jnp.logical_or(up_iface, down_iface)
    has_up = z < n_z - 1
    has_down = z > 0
    send_up = jnp.logical_and(has_up, jnp.logical_not(up_iface))
    send_down = jnp.logical_and(has_down, jnp.logical_not(down_iface))
    s_face = 2 * jnp.where(up_iface, z + 1, z - 1)
    p_left = lax.rem(p + n_span - 1, n_span)
    p_right = lax.rem(p + 1, n_span)
    s_pair = s + 1 - 2 * h
    partner = {"stream": s_pair, "span": p}
    above = {"stream": lax.rem(s + 2, n_stream), "span": p}
    below = {"stream": lax.rem(s + n_stream - 2, n_stream), "span": p}

    def count(flag):
        return jnp.where(flag, 1, 0)

    def half(i):
        return pl.ds(pl.multiple_of(i * HALF, HALF), HALF)

    def mine(k):
        return jnp.where(k == 2, 2, 3 * h + k)

    def theirs(k):
        return jnp.where(k == 2, 2, 3 - 3 * h + k)

    def at(st, k):
        return jnp.where(h == st, mine(k), NC + k)

    def side_of(k, q):
        return jnp.where(k == 2, lax.rem(q, 2), h)

    def remote(src, dst, send, recv, device):
        return pltpu.make_async_remote_copy(
            src_ref=src, dst_ref=dst, send_sem=send, recv_sem=recv, device_id=device, device_id_type=MESH
        )

    local_ck = pltpu.make_async_copy(ck_h, cx.at[pl.ds(0, NC)], l_sem.at[0])
    local_adj = pltpu.make_async_copy(adj_h, adj, l_sem.at[1])
    local_li = pltpu.make_async_copy(li_h, li, l_sem.at[2])
    local_rs = pltpu.make_async_copy(rs_h, rs, l_sem.at[3])

    def send_ck(k):
        return remote(ck_h.at[theirs(k)], cx.at[NC + k], ck_s.at[k], ck_r.at[k], partner)

    def send_ca(k):
        return remote(cb.at[theirs(k)], cb.at[NC + k], ca_s.at[k], ca_r.at[k], partner)

    def send_out(k, c):
        return remote(ob.at[k], o_ref.at[c], o_s.at[k], o_r.at[k], partner)

    def field_up(f, k):
        return remote(fld.at[f, 2, k], fld.at[f, 0, k], z_s.at[f, k, 0], z_r.at[f, k, 0], above)

    def field_down(f, k):
        return remote(fld.at[f, 1, k], fld.at[f, 3, k], z_s.at[f, k, 1], z_r.at[f, k, 1], below)

    def own_edge(c, side):
        q = (p_right, p_left)[side]
        row = pl.ds(1 - side, 1)
        owner = jnp.where(c == 2, lax.rem(q, 2), c // 3)
        k = jnp.where(c > 2, c - 3, c)
        return remote(
            eo.at[c, row], er.at[0, k, h, row], eo_s.at[c, side], eo_r.at[k, side, h],
            {"stream": s - h + owner, "span": q},
        )

    def own_edge_in(k, side, st):
        row = pl.ds(1 - side, 1)
        return remote(eo.at[k, row], er.at[0, k, st, row], eo_s.at[k, side], eo_r.at[k, side, st], partner)

    def edge(k, side):
        row = pl.ds(1 - side, 1)
        q = (p_right, p_left)[side]
        return remote(
            es.at[k, :, row], er.at[1, k, :, row], e_s.at[k, side], e_r.at[k, side],
            {"stream": s - h + side_of(k, q), "span": q},
        )

    sent = pl.ds(0, cap)

    def face(f, k, j):
        return remote(
            ys.at[f, k, j, sent], yr.at[f, k, p, sent], i_s.at[f, k], i_r.at[f, k],
            {"stream": s_face + side_of(k, j), "span": j},
        )

    def face_all(f, k):
        return remote(ys.at[f, k, :, sent], yr.at[f, k, :, sent], i_s.at[f, k], i_r.at[f, k], partner)

    local_rs.start()
    local_ck.start()
    local_adj.start()
    local_li.start()

    barrier = pltpu.get_barrier_semaphore()

    def greet(semaphore, stream, span):
        device = {"stream": stream, "span": span}
        pl.semaphore_signal(semaphore, inc=1, device_id=device, device_id_type=MESH)

    def greet_face(semaphore):
        @pl.loop(0, n_span)
        def _(j):
            greet(semaphore, s_face + h, j)

        @pl.when(slots == 3)
        def _():
            @pl.loop(0, n_span // 2)
            def _(j):
                greet(semaphore, s_face + 1 - h, 2 * j + 1 - h)

    greet(barrier, s_pair, p)
    for stream in (s, s_pair):
        greet(barrier, stream, p_left)
        greet(barrier, stream, p_right)

    @pl.when(send_up)
    def _():
        greet(barrier, above["stream"], p)

    @pl.when(up_iface)
    def _():
        greet_face(barrier)

    met = n_span + (slots - 2) * (n_span // 2)


    zero = jnp.zeros((NL, CP), F32)

    @pl.when(jnp.logical_not(has_down))
    def _():
        for f in range(2):
            for k in range(3):
                fld[f, 0, k] = zero

    @pl.when(jnp.logical_not(has_up))
    def _():
        for f in range(2):
            for k in range(3):
                fld[f, 3, k] = zero

    local_rs.wait()

    @pl.when(iface)
    def _():
        rows = rs.shape[0]
        source = rs[...]
        ids = lax.broadcasted_iota(I32, (rows, CP), 0) * CP + lax.broadcasted_iota(I32, (rows, CP), 1)
        rotor = jnp.broadcast_to(count(up_iface), (rows, CP)) == 1
        own = jnp.where(rotor, source, ids)
        far = jnp.where(rotor, ids, source)
        local = div_rows(own) == p
        order = jnp.where(rotor, div_rows(far) * NL + own - p * NL, far)
        order = jnp.where(local, order, 1 << 20)
        row = lax.broadcasted_iota(I32, (NL, CP), 0)
        total = jnp.zeros((NL, CP), I32)
        for i in range(rows):
            total = total + jnp.where(own[i:i + 1, :] == row + p * NL, far[i:i + 1, :], 0)
        link = jnp.sum(total.astype(F32), axis=1, keepdims=True).astype(I32)
        rotor_col = jnp.broadcast_to(count(up_iface), (NL, 1)) == 1
        row_col = lax.broadcasted_iota(I32, (NL, 1), 0)
        key = jnp.where(rotor_col, div_rows(link) * NL + row_col, link)
        keys = jnp.broadcast_to(key, (NL, CP))
        total = jnp.zeros((NL, CP), I32)
        for i in range(rows):
            total = total + jnp.where(order[i:i + 1, :] < keys, 1, 0)
        place = jnp.sum(total.astype(F32), axis=1, keepdims=True).astype(I32)
        place = place + (pad - cap) * div_rows(link)
        lanes = lax.broadcasted_iota(I32, tm.shape, 1)
        tm[...] = jnp.where(jnp.broadcast_to(place, tm.shape) == lanes, 1.0, 0.0).astype(BF16)
        same = lax.broadcasted_iota(I32, (NL, NL), 0) == lax.broadcasted_iota(I32, (NL, NL), 1)
        tmt[...] = dot(tm[...], jnp.where(same, 1.0, 0.0).astype(BF16), ((0,), (0,))).astype(BF16)

    pl.semaphore_wait(barrier, 5 + jnp.where(down_iface, met, count(send_down)))

    @pl.loop(0, other_slots)
    def _(k):
        send_ck(k).start()

    @pl.when(send_down)
    def _():
        greet(ready, below["stream"], p)

    @pl.when(down_iface)
    def _():
        greet_face(ready)

    sel_row = lax.broadcasted_iota(I32, (16, CP), 0)
    sel_lane = lax.broadcasted_iota(I32, (16, CP), 1)
    first, last = sel_lane == 0, sel_lane == CP - 1
    take = jnp.logical_or(jnp.logical_and(sel_row == 0, first), jnp.logical_and(sel_row == 1, last))
    take = jnp.where(take, 1.0, 0.0).astype(BF16)
    give = jnp.where(sel_row < 2, jnp.where(first, 1.0, 0.0), jnp.where(last, 1.0, 0.0))
    give = jnp.where(sel_row < 4, give, 0.0).astype(BF16)

    def edges_of(x):
        hi, lo = split(x)
        return dot(jnp.concatenate([take, take], axis=1), jnp.concatenate([hi, lo], axis=1), ((1,), (1,)))[0:8]

    def scatter_rows(x):
        hi, lo = split(x)
        t = tmt[...]
        y = dot(t, jnp.concatenate([hi, lo], axis=1), ((1,), (0,)))
        return (y[:, :CP] + y[:, CP:]).reshape(n_span, pad, CP)

    local_ck.wait()

    @pl.loop(0, NC)
    def _(c):
        fo[c] = jnp.tanh(cx[c])

    early_up = jnp.logical_and(send_up, h == 1)

    @pl.when(early_up)
    def _():
        pl.semaphore_wait(ready, 1)

    @pl.loop(0, slots)
    def _(k):
        fld[0, h + 1, k] = fo[mine(k)]

        @pl.when(early_up)
        def _():
            field_up(0, k).start()

        @pl.when(jnp.logical_and(send_down, h == 0))
        def _():
            field_down(0, k).start()

    @pl.loop(0, NC)
    def _(c):
        eo[c] = edges_of(fo[c])
        own_edge(c, 0).start()
        own_edge(c, 1).start()

    def send_face(f, k, st):
        ys[f, k] = scatter_rows(fld[f, st + 1, k])

        for j in range(n_span):
            face(f, k, j).start()

    local_adj.wait()
    local_li.wait()
    for b in range(NB):
        rhs = jnp.concatenate([adj[c, b * LB:(b + 1) * LB, :] for c in range(NC)], axis=0).astype(BF16)
        carried = dot(li[b], rhs, ((0,), (0,)))
        for e in range(NC):
            cb[e, b * LB:(b + 1) * LB, :] = carried[e * LB:(e + 1) * LB, :]

    def receive_field(f, k):
        for side in range(2):
            if f == 0:
                own_edge_in(k, side, 0).wait_recv()
                own_edge_in(k, side, 1).wait_recv()
            else:
                edge(k, side).wait_recv()
        r = lax.broadcasted_iota(I32, (16, NL), 0)
        for st in range(2):
            from_left = jnp.broadcast_to(er[f, k, st, 1:2, :], r.shape)
            from_right = jnp.broadcast_to(er[f, k, st, 0:1, :], r.shape)
            v = jnp.where(r < 2, from_left, from_right)
            hi = v.astype(BF16).astype(F32)
            v = jnp.where(lax.rem(r, 2) == 0, hi, v - hi)
            v = jnp.where(r < 4, v, 0.0).astype(BF16)
            hb[st] = dot(v, give, ((0,), (0,)))

        @pl.when(iface)
        def _():
            face_all(f, k).wait_recv()
            held = jnp.where(lax.broadcasted_iota(I32, (n_span, pad, CP), 1) < cap, yr[f, k], 0.0)
            hi, lo = split(held.reshape(n_span * pad, CP))
            t = tm[...]
            y = dot(t, jnp.concatenate([hi, lo], axis=1), ((1,), (0,)))
            fld[f, 3 * count(up_iface), k] = y[:, :CP] + y[:, CP:]

        @pl.when(send_down)
        def _():
            field_up(f, k).wait_recv()

        @pl.when(send_up)
        def _():
            field_down(f, k).wait_recv()

    lane = lax.broadcasted_iota(I32, (HALF, CP), 1)

    def stencil(f, st, k, r, coef_down, coef_up, center, lateral):
        x = fld[f, st + 1, k, r]
        up = fld[f, st, k, r]
        down = fld[f, st + 2, k, r]
        sides = jnp.where(lane == 0, 0.0, pltpu.roll(x, 1, 1)) + jnp.where(lane == CP - 1, 0.0, pltpu.roll(x, CP - 1, 1))
        sides = sides + hb[st, r] - 2.0 * x
        return x, coef_down * down + coef_up * up + center * x + lateral * sides

    def coefs(k):
        c = mine(k)
        advect = pick(ADVECTION, c)
        dissip = pick(DISSIPATION, c)
        return -0.5 * advect + dissip, 0.5 * advect + dissip, -2.0 * dissip, pick(SPREADING, c)

    def flux_step(k):
        send_ck(k).wait_recv()
        fld[0, 2 - h, k] = jnp.tanh(cx[NC + k])

        @pl.when(jnp.logical_and(send_up, h == 0))
        def _():
            field_up(0, k).start()

        @pl.when(jnp.logical_and(send_down, h == 1))
        def _():
            field_down(0, k).start()

        @pl.when(iface)
        def _():
            send_face(0, k, count(up_iface))

    def slope_step(k):
        down_c, up_c, center, lateral = coefs(k)
        receive_field(0, k)

        @pl.loop(0, 2)
        def _(i):
            r = half(i)
            for st in range(2):
                _, op = stencil(0, st, k, r, down_c, up_c, center, lateral)
                t = jnp.tanh(cx[at(st, k), r] + time_step * op)
                fld[1, st + 1, k, r] = 2.0 - t * t

    def weight_step(k):
        send_ca(k).wait_recv()
        for st in range(2):
            fld[1, st + 1, k] = fld[1, st + 1, k] * cb[at(st, k)]

        @pl.when(send_up)
        def _():
            field_up(1, k).start()

        @pl.when(send_down)
        def _():
            field_down(1, k).start()

        @pl.when(iface)
        def _():
            send_face(1, k, count(up_iface))

        for st in range(2):
            es[k, st] = edges_of(fld[1, st + 1, k])
        edge(k, 0).start()
        edge(k, 1).start()

    def result_step(k):
        down_c, up_c, center, lateral = coefs(k)
        receive_field(1, k)

        def result(st, r):
            w, op = stencil(1, st, k, r, up_c, down_c, center, lateral)
            x = fld[0, st + 1, k, r]
            return w + time_step * (1.0 - x * x) * op

        @pl.loop(0, 2)
        def _(i):
            ob[k, half(i)] = result(1 - h, half(i))

        send_out(k, mine(k)).start()

        @pl.loop(0, 2)
        def _(i):
            o_ref[mine(k), half(i)] = result(h, half(i))

    @pl.when(jnp.logical_and(send_up, h == 0))
    def _():
        pl.semaphore_wait(ready, 1)

    @pl.when(up_iface)
    def _():
        pl.semaphore_wait(ready, met)

    @pl.loop(0, slots)
    def _(t):
        flux_step(t)

        @pl.when(t == 0)
        def _():
            @pl.loop(0, other_slots)
            def _(k):
                send_ca(k).start()

    @pl.loop(0, slots)
    def _(k):
        slope_step(k)
        weight_step(k)

    pl.loop(0, slots)(result_step)

    @pl.loop(0, other_slots)
    def _(k):
        send_ck(k).wait_send()
        send_ca(k).wait_send()
        send_out(k, theirs(k)).wait_recv()

    @pl.loop(0, NC)
    def _(c):
        own_edge(c, 0).wait_send()
        own_edge(c, 1).wait_send()

    @pl.loop(0, slots)
    def _(k):
        send_out(k, mine(k)).wait_send()
        edge(k, 0).wait_send()
        edge(k, 1).wait_send()
        for f in range(2):
            @pl.when(send_up)
            def _():
                field_up(f, k).wait_send()

            @pl.when(send_down)
            def _():
                field_down(f, k).wait_send()

        @pl.when(iface)
        def _():
            face_all(0, k).wait_send()
            face_all(1, k).wait_send()


def solution(mesh):
    n_stream, n_span = mesh.shape["stream"], mesh.shape["span"]

    def local(checkpoint, adjoint, line_inverse, row_source):
        pad = -(-(NL // n_span) // 8) * 8
        dma = pltpu.SemaphoreType.DMA
        shape = (NL, CP)

        def body(*refs):
            kernel(n_stream, n_span, *refs)

        operands = (
            checkpoint.reshape(NC, NL, CP),
            adjoint.reshape(NC, NL, CP),
            line_inverse.reshape(NB, NC * LB, NC * LB),
            row_source.reshape(-1, CP),
        )
        out = pl.pallas_call(
            body,
            out_shape=jax.ShapeDtypeStruct((NC, NL, CP), F32),
            in_specs=[pl.BlockSpec(memory_space=pltpu.HBM)] * 4,
            out_specs=pl.BlockSpec(memory_space=pltpu.VMEM),
            scratch_shapes=[
                pltpu.VMEM((NC + 3,) + shape, F32),
                pltpu.VMEM((NC,) + shape, F32),
                pltpu.VMEM((NB, NC * LB, NC * LB), BF16),
                pltpu.VMEM((row_source.size // CP, CP), I32),
                pltpu.VMEM((NC + 3,) + shape, F32),
                pltpu.VMEM((NC,) + shape, F32),
                pltpu.VMEM((2, 4, 3) + shape, F32),
                pltpu.VMEM((2,) + shape, F32),
                pltpu.VMEM((3,) + shape, F32),
                pltpu.VMEM((NC, 8, NL), F32),
                pltpu.VMEM((3, 2, 8, NL), F32),
                pltpu.VMEM((2, 3, 2, 8, NL), F32),
                pltpu.VMEM((2, 3, n_span, pad, CP), F32),
                pltpu.VMEM((2, 3, n_span, pad, CP), F32),
                pltpu.VMEM((NL, n_span * pad), BF16),
                pltpu.VMEM((n_span * pad, NL), BF16),
                dma((4,)), dma((3,)), dma((3,)), dma((3,)), dma((3,)),
                dma((2, 3, 2)), dma((2, 3, 2)), dma((2, 3)), dma((2, 3)),
                dma((NC, 2)), dma((3, 2, 2)), dma((3, 2)), dma((3, 2)), dma((3,)), dma((3,)),
                pltpu.SemaphoreType.REGULAR,
            ],
            compiler_params=pltpu.CompilerParams(
                collective_id=0, has_side_effects=True, vmem_limit_bytes=48 << 20
            ),
            name="adjoint_step",
        )(
            *(pltpu.with_memory_space_constraint(x, pltpu.HBM) for x in operands)
        )
        return out.reshape(NC, NL, 1, CP)

    return jax.shard_map(
        local,
        mesh=mesh,
        in_specs=(
            P(None, None, "stream", "span"),
            P(None, None, "stream", "span"),
            P("stream", None, None, None),
            P(),
        ),
        out_specs=P(None, None, "stream", "span"),
        check_vma=False,
    )
```

time: 161 us -> 36 us (0.22)
  the two profiles are of different devices: /device:TPU:4 before, /device:TPU:228 now
where the time goes in v1:
time: 36 us; the launch traced here: 35.9 us
  Pallas kernels  35.1 us (98%)
  local copies, waits for them, and re-layouts  0.78 us (2%)
    pallas_call x1, Pallas kernels, local(): pl.pallas_call(body, out_shape=jax.ShapeDtypeStruct((NC, NL, CP), F32), i...  35.1 us
    unnamed x1, local copies, waits for them, and re-layouts  0.78 us

profile of v1, /device:TPU:228, one launch (start us, length us, event | category | flops | bytes accessed | tf_op | source)
XLA Modules:
  0.0 35.9 jit_solution(15728504981379204309)
XLA Ops:
  0.0 35.1 %adjoint_step.1 = f32[5,192,128]{2,1,0:T(8,128)S(1)} custom-call(f32[5,192,128]{2,1,0:T(8,128)} %bitcast.9, f32[5,192,128]{2,1,0:T(8,128)} %bitcast.10, bf16[3,320,320]{2,1,0:T(8,128)(2,1)} %bitcast.8, s32[24,128]{1,0:T(8,128)} %bitcast.11), custom_call_target="tpu_custom_call" | custom-call | tf_op jit(solution)/shard_map/adjoint_step/pallas_call | solution.py:496
  35.1 0.8 %copy.7 = f32[5,192,1,128]{3,2,1,0:T(1,128)} copy(f32[5,192,1,128]{3,2,1,0:T(1,128)S(1)} %bitcast.7) | data formatting | bytes 983040

commit v2 on v1

--- a/solution.py
+++ b/solution.py
@@ -38,7 +38,7 @@
 def kernel(
     n_stream, n_span, ck_h, adj_h, li_h, rs_h, o_ref,
     cx, adj, li, rs, cb, fo, fld, hb, ob, eo, es, er, ys, yr, tm, tmt,
-    l_sem, ck_s, ck_r, ca_s, ca_r, z_s, z_r, i_s, i_r, eo_s, eo_r, e_s, e_r, o_s, o_r, ready,
+    l_sem, ck_s, ck_r, ca_s, ca_r, z_s, z_r, i_s, i_r, eo_s, eo_r, e_s, e_r, o_s, o_r, ready, beside,
 ):
     s = lax.axis_index("stream")
     p = lax.axis_index("span")
@@ -99,8 +99,8 @@
     def send_ca(k):
         return remote(cb.at[theirs(k)], cb.at[NC + k], ca_s.at[k], ca_r.at[k], partner)
 
-    def send_out(k, c):
-        return remote(ob.at[k], o_ref.at[c], o_s.at[k], o_r.at[k], partner)
+    def send_out(k, c, i):
+        return remote(ob.at[k, half(i)], o_ref.at[c, half(i)], o_s.at[k, i], o_r.at[k, i], partner)
 
     def field_up(f, k):
         return remote(fld.at[f, 2, k], fld.at[f, 0, k], z_s.at[f, k, 0], z_r.at[f, k, 0], above)
@@ -163,10 +163,21 @@
             def _(j):
                 greet(semaphore, s_face + 1 - h, 2 * j + 1 - h)
 
+    def greet_tile(semaphore, q):
+        greet(semaphore, s, q)
+        greet(semaphore, s_pair, q)
+
+    first_tile = p == 0
+    last_tile = p == n_span - 1
     greet(barrier, s_pair, p)
-    for stream in (s, s_pair):
-        greet(barrier, stream, p_left)
-        greet(barrier, stream, p_right)
+
+    @pl.when(jnp.logical_not(last_tile))
+    def _():
+        greet_tile(barrier, p_right)
+
+    @pl.when(first_tile)
+    def _():
+        greet_tile(barrier, p_left)
 
     @pl.when(send_up)
     def _():
@@ -192,6 +203,60 @@
         for f in range(2):
             for k in range(3):
                 fld[f, 3, k] = zero
+
+    sel_row = lax.broadcasted_iota(I32, (16, CP), 0)
+    sel_lane = lax.broadcasted_iota(I32, (16, CP), 1)
+    first, last = sel_lane == 0, sel_lane == CP - 1
+    take = jnp.logical_or(jnp.logical_and(sel_row == 0, first), jnp.logical_and(sel_row == 1, last))
+    take = jnp.where(take, 1.0, 0.0).astype(BF16)
+    give = jnp.where(sel_row < 2, jnp.where(first, 1.0, 0.0), jnp.where(last, 1.0, 0.0))
+    give = jnp.where(sel_row < 4, give, 0.0).astype(BF16)
+
+    def edges_of(x):
+        hi, lo = split(x)
+        return dot(jnp.concatenate([take, take], axis=1), jnp.concatenate([hi, lo], axis=1), ((1,), (1,)))[0:8]
+
+    def scatter_rows(x):
+        hi, lo = split(x)
+        t = tmt[...]
+        y = dot(t, jnp.concatenate([hi, lo], axis=1), ((1,), (0,)))
+        return (y[:, :CP] + y[:, CP:]).reshape(n_span, pad, CP)
+
+    lower = jnp.where(first_tile, 0, jnp.where(last_tile, 4, 2))
+    pl.semaphore_wait(barrier, 1 + lower + jnp.where(down_iface, met, count(send_down)))
+
+    @pl.when(send_down)
+    def _():
+        greet(ready, below["stream"], p)
+
+    send_ck(0).start()
+    send_ck(1).start()
+
+    @pl.when(down_iface)
+    def _():
+        greet_face(ready)
+
+    @pl.when(jnp.logical_not(first_tile))
+    def _():
+        greet_tile(beside, p_left)
+
+    @pl.when(last_tile)
+    def _():
+        greet_tile(beside, p_right)
+
+    @pl.when(other_slots == 3)
+    def _():
+        send_ck(2).start()
+
+    local_ck.wait()
+
+    @pl.loop(0, NC)
+    def _(c):
+        fo[c] = jnp.tanh(cx[c])
+
+    @pl.loop(0, NC)
+    def _(c):
+        eo[c] = edges_of(fo[c])
 
     local_rs.wait()
 
@@ -225,67 +290,13 @@
         same = lax.broadcasted_iota(I32, (NL, NL), 0) == lax.broadcasted_iota(I32, (NL, NL), 1)
         tmt[...] = dot(tm[...], jnp.where(same, 1.0, 0.0).astype(BF16), ((0,), (0,))).astype(BF16)
 
-    pl.semaphore_wait(barrier, 5 + jnp.where(down_iface, met, count(send_down)))
-
-    @pl.loop(0, other_slots)
-    def _(k):
-        send_ck(k).start()
-
-    @pl.when(send_down)
-    def _():
-        greet(ready, below["stream"], p)
-
-    @pl.when(down_iface)
-    def _():
-        greet_face(ready)
-
-    sel_row = lax.broadcasted_iota(I32, (16, CP), 0)
-    sel_lane = lax.broadcasted_iota(I32, (16, CP), 1)
-    first, last = sel_lane == 0, sel_lane == CP - 1
-    take = jnp.logical_or(jnp.logical_and(sel_row == 0, first), jnp.logical_and(sel_row == 1, last))
-    take = jnp.where(take, 1.0, 0.0).astype(BF16)
-    give = jnp.where(sel_row < 2, jnp.where(first, 1.0, 0.0), jnp.where(last, 1.0, 0.0))
-    give = jnp.where(sel_row < 4, give, 0.0).astype(BF16)
-
-    def edges_of(x):
-        hi, lo = split(x)
-        return dot(jnp.concatenate([take, take], axis=1), jnp.concatenate([hi, lo], axis=1), ((1,), (1,)))[0:8]
-
-    def scatter_rows(x):
-        hi, lo = split(x)
-        t = tmt[...]
-        y = dot(t, jnp.concatenate([hi, lo], axis=1), ((1,), (0,)))
-        return (y[:, :CP] + y[:, CP:]).reshape(n_span, pad, CP)
-
-    local_ck.wait()
-
-    @pl.loop(0, NC)
-    def _(c):
-        fo[c] = jnp.tanh(cx[c])
-
-    early_up = jnp.logical_and(send_up, h == 1)
-
-    @pl.when(early_up)
-    def _():
-        pl.semaphore_wait(ready, 1)
-
     @pl.loop(0, slots)
     def _(k):
         fld[0, h + 1, k] = fo[mine(k)]
 
-        @pl.when(early_up)
-        def _():
-            field_up(0, k).start()
-
         @pl.when(jnp.logical_and(send_down, h == 0))
         def _():
             field_down(0, k).start()
-
-    @pl.loop(0, NC)
-    def _(c):
-        eo[c] = edges_of(fo[c])
-        own_edge(c, 0).start()
-        own_edge(c, 1).start()
 
     def send_face(f, k, st):
         ys[f, k] = scatter_rows(fld[f, st + 1, k])
@@ -300,6 +311,15 @@
         carried = dot(li[b], rhs, ((0,), (0,)))
         for e in range(NC):
             cb[e, b * LB:(b + 1) * LB, :] = carried[e * LB:(e + 1) * LB, :]
+
+    @pl.when(jnp.logical_not(last_tile))
+    def _():
+        pl.semaphore_wait(beside, jnp.where(first_tile, 4, 2))
+
+    @pl.loop(0, NC)
+    def _(c):
+        own_edge(c, 0).start()
+        own_edge(c, 1).start()
 
     def receive_field(f, k):
         for side in range(2):
@@ -355,16 +375,24 @@
         send_ck(k).wait_recv()
         fld[0, 2 - h, k] = jnp.tanh(cx[NC + k])
 
+        @pl.when(jnp.logical_and(send_down, h == 1))
+        def _():
+            field_down(0, k).start()
+
         @pl.when(jnp.logical_and(send_up, h == 0))
         def _():
+            @pl.when(k == 0)
+            def _():
+                pl.semaphore_wait(ready, 1)
+
             field_up(0, k).start()
 
-        @pl.when(jnp.logical_and(send_down, h == 1))
-        def _():
-            field_down(0, k).start()
-
         @pl.when(iface)
         def _():
+            @pl.when(jnp.logical_and(up_iface, k == 0))
+            def _():
+                pl.semaphore_wait(ready, met)
+
             send_face(0, k, count(up_iface))
 
     def slope_step(k):
@@ -413,26 +441,25 @@
         @pl.loop(0, 2)
         def _(i):
             ob[k, half(i)] = result(1 - h, half(i))
-
-        send_out(k, mine(k)).start()
+            send_out(k, mine(k), i).start()
 
         @pl.loop(0, 2)
         def _(i):
             o_ref[mine(k), half(i)] = result(h, half(i))
 
-    @pl.when(jnp.logical_and(send_up, h == 0))
+    @pl.when(jnp.logical_and(send_up, h == 1))
     def _():
         pl.semaphore_wait(ready, 1)
 
-    @pl.when(up_iface)
-    def _():
-        pl.semaphore_wait(ready, met)
+        @pl.loop(0, slots)
+        def _(k):
+            field_up(0, k).start()
 
     @pl.loop(0, slots)
     def _(t):
         flux_step(t)
 
-        @pl.when(t == 0)
+        @pl.when(t == count(jnp.logical_and(iface, h == 1)) * (slots - 2))
         def _():
             @pl.loop(0, other_slots)
             def _(k):
@@ -449,7 +476,8 @@
     def _(k):
         send_ck(k).wait_send()
         send_ca(k).wait_send()
-        send_out(k, theirs(k)).wait_recv()
+        send_out(k, theirs(k), 0).wait_recv()
+        send_out(k, theirs(k), 1).wait_recv()
 
     @pl.loop(0, NC)
     def _(c):
@@ -458,7 +486,8 @@
 
     @pl.loop(0, slots)
     def _(k):
-        send_out(k, mine(k)).wait_send()
+        send_out(k, mine(k), 0).wait_send()
+        send_out(k, mine(k), 1).wait_send()
         edge(k, 0).wait_send()
         edge(k, 1).wait_send()
         for f in range(2):
@@ -517,8 +546,8 @@
                 pltpu.VMEM((n_span * pad, NL), BF16),
                 dma((4,)), dma((3,)), dma((3,)), dma((3,)), dma((3,)),
                 dma((2, 3, 2)), dma((2, 3, 2)), dma((2, 3)), dma((2, 3)),
-                dma((NC, 2)), dma((3, 2, 2)), dma((3, 2)), dma((3, 2)), dma((3,)), dma((3,)),
-                pltpu.SemaphoreType.REGULAR,
+                dma((NC, 2)), dma((3, 2, 2)), dma((3, 2)), dma((3, 2)), dma((3, 2)), dma((3, 2)),
+                pltpu.SemaphoreType.REGULAR, pltpu.SemaphoreType.REGULAR,
             ],
             compiler_params=pltpu.CompilerParams(
                 collective_id=0, has_side_effects=True, vmem_limit_bytes=48 << 20

time: 36 us -> 35.7 us (level)
  the two profiles are of different devices: /device:TPU:228 before, /device:TPU:225 now
where the time goes in v2:
time: 35.7 us; the launch traced here: 35.6 us
  Pallas kernels  34.8 us (97%)
  local copies, waits for them, and re-layouts  0.78 us (2%)
    pallas_call x1, Pallas kernels, local(): pl.pallas_call(body, out_shape=jax.ShapeDtypeStruct((NC, NL, CP), F32), i...  34.8 us
    unnamed x1, local copies, waits for them, and re-layouts  0.78 us

profile of v2, /device:TPU:225, one launch (start us, length us, event | category | flops | bytes accessed | tf_op | source)
XLA Modules:
  0.0 35.6 jit_solution(11909767575610795009)
XLA Ops:
  0.0 34.8 %adjoint_step.1 = f32[5,192,128]{2,1,0:T(8,128)S(1)} custom-call(f32[5,192,128]{2,1,0:T(8,128)} %bitcast.9, f32[5,192,128]{2,1,0:T(8,128)} %bitcast.10, bf16[3,320,320]{2,1,0:T(8,128)(2,1)} %bitcast.8, s32[24,128]{1,0:T(8,128)} %bitcast.11), custom_call_target="tpu_custom_call" | custom-call | tf_op jit(solution)/shard_map/adjoint_step/pallas_call | solution.py:525
  34.8 0.8 %copy.7 = f32[5,192,1,128]{3,2,1,0:T(1,128)} copy(f32[5,192,1,128]{3,2,1,0:T(1,128)S(1)} %bitcast.7) | data formatting | bytes 983040

commit v3 on v2

--- a/solution.py
+++ b/solution.py
@@ -141,54 +141,53 @@
     def face_all(f, k):
         return remote(ys.at[f, k, :, sent], yr.at[f, k, :, sent], i_s.at[f, k], i_r.at[f, k], partner)
 
+    barrier = pltpu.get_barrier_semaphore()
+
+    def greet(semaphore, stream, span):
+        device = {"stream": stream, "span": span}
+        pl.semaphore_signal(semaphore, inc=1, device_id=device, device_id_type=MESH)
+
+    def greet_face(semaphore):
+        for j in range(n_span):
+            greet(semaphore, s_face + h, j)
+
+        @pl.when(slots == 3)
+        def _():
+            @pl.loop(0, n_span // 2)
+            def _(j):
+                greet(semaphore, s_face + 1 - h, 2 * j + 1 - h)
+
+    def greet_tile(semaphore, q):
+        greet(semaphore, s, q)
+        greet(semaphore, s_pair, q)
+
+    first_tile = p == 0
+    last_tile = p == n_span - 1
+    greet(barrier, s_pair, p)
+
+    @pl.when(up_iface)
+    def _():
+        greet_face(barrier)
+
+    @pl.when(jnp.logical_not(last_tile))
+    def _():
+        greet_tile(barrier, p_right)
+
+    @pl.when(first_tile)
+    def _():
+        greet_tile(barrier, p_left)
+
+    @pl.when(send_up)
+    def _():
+        greet(barrier, above["stream"], p)
+
+    met = n_span + (slots - 2) * (n_span // 2)
+
+
     local_rs.start()
     local_ck.start()
     local_adj.start()
     local_li.start()
-
-    barrier = pltpu.get_barrier_semaphore()
-
-    def greet(semaphore, stream, span):
-        device = {"stream": stream, "span": span}
-        pl.semaphore_signal(semaphore, inc=1, device_id=device, device_id_type=MESH)
-
-    def greet_face(semaphore):
-        @pl.loop(0, n_span)
-        def _(j):
-            greet(semaphore, s_face + h, j)
-
-        @pl.when(slots == 3)
-        def _():
-            @pl.loop(0, n_span // 2)
-            def _(j):
-                greet(semaphore, s_face + 1 - h, 2 * j + 1 - h)
-
-    def greet_tile(semaphore, q):
-        greet(semaphore, s, q)
-        greet(semaphore, s_pair, q)
-
-    first_tile = p == 0
-    last_tile = p == n_span - 1
-    greet(barrier, s_pair, p)
-
-    @pl.when(jnp.logical_not(last_tile))
-    def _():
-        greet_tile(barrier, p_right)
-
-    @pl.when(first_tile)
-    def _():
-        greet_tile(barrier, p_left)
-
-    @pl.when(send_up)
-    def _():
-        greet(barrier, above["stream"], p)
-
-    @pl.when(up_iface)
-    def _():
-        greet_face(barrier)
-
-    met = n_span + (slots - 2) * (n_span // 2)
-
 
     zero = jnp.zeros((NL, CP), F32)
 
@@ -225,16 +224,16 @@
     lower = jnp.where(first_tile, 0, jnp.where(last_tile, 4, 2))
     pl.semaphore_wait(barrier, 1 + lower + jnp.where(down_iface, met, count(send_down)))
 
+    @pl.when(down_iface)
+    def _():
+        greet_face(ready)
+
     @pl.when(send_down)
     def _():
         greet(ready, below["stream"], p)
 
     send_ck(0).start()
     send_ck(1).start()
-
-    @pl.when(down_iface)
-    def _():
-        greet_face(ready)
 
     @pl.when(jnp.logical_not(first_tile))
     def _():

time: 35.7 us -> 35.7 us (level)
  no operation moved by 1% of the time
where the time goes in v3:
time: 35.7 us; the launch traced here: 35.6 us
  Pallas kernels  34.8 us (97%)
  local copies, waits for them, and re-layouts  0.78 us (2%)
    pallas_call x1, Pallas kernels, local(): pl.pallas_call(body, out_shape=jax.ShapeDtypeStruct((NC, NL, CP), F32), i...  34.8 us
    unnamed x1, local copies, waits for them, and re-layouts  0.78 us

profile of v3, /device:TPU:225, one launch (start us, length us, event | category | flops | bytes accessed | tf_op | source)
XLA Modules:
  0.0 35.6 jit_solution(18369521484365556495)
XLA Ops:
  0.0 34.8 %adjoint_step.1 = f32[5,192,128]{2,1,0:T(8,128)S(1)} custom-call(f32[5,192,128]{2,1,0:T(8,128)} %bitcast.9, f32[5,192,128]{2,1,0:T(8,128)} %bitcast.10, bf16[3,320,320]{2,1,0:T(8,128)(2,1)} %bitcast.8, s32[24,128]{1,0:T(8,128)} %bitcast.11), custom_call_target="tpu_custom_call" | custom-call | tf_op jit(solution)/shard_map/adjoint_step/pallas_call | solution.py:524
  34.8 0.8 %copy.7 = f32[5,192,1,128]{3,2,1,0:T(1,128)} copy(f32[5,192,1,128]{3,2,1,0:T(1,128)S(1)} %bitcast.7) | data formatting | bytes 983040

commit v4 on v2

--- a/solution.py
+++ b/solution.py
@@ -122,11 +122,11 @@
         row = pl.ds(1 - side, 1)
         return remote(eo.at[k, row], er.at[0, k, st, row], eo_s.at[k, side], eo_r.at[k, side, st], partner)
 
-    def edge(k, side):
+    def edge(k, side, st):
         row = pl.ds(1 - side, 1)
         q = (p_right, p_left)[side]
         return remote(
-            es.at[k, :, row], er.at[1, k, :, row], e_s.at[k, side], e_r.at[k, side],
+            es.at[k, st, row], er.at[1, k, st, row], e_s.at[k, side, st], e_r.at[k, side, st],
             {"stream": s - h + side_of(k, q), "span": q},
         )
 
@@ -323,11 +323,9 @@
 
     def receive_field(f, k):
         for side in range(2):
-            if f == 0:
-                own_edge_in(k, side, 0).wait_recv()
-                own_edge_in(k, side, 1).wait_recv()
-            else:
-                edge(k, side).wait_recv()
+            for st in range(2):
+                message = edge(k, side, st) if f else own_edge_in(k, side, st)
+                message.wait_recv()
         r = lax.broadcasted_iota(I32, (16, NL), 0)
         for st in range(2):
             from_left = jnp.broadcast_to(er[f, k, st, 1:2, :], r.shape)
@@ -407,27 +405,28 @@
                 t = jnp.tanh(cx[at(st, k), r] + time_step * op)
                 fld[1, st + 1, k, r] = 2.0 - t * t
 
-    def weight_step(k):
+    def weight_step(k, st):
+        fld[1, st + 1, k] = fld[1, st + 1, k] * cb[at(st, k)]
+
+        @pl.when(jnp.logical_and(send_up, st == 1))
+        def _():
+            field_up(1, k).start()
+
+        @pl.when(jnp.logical_and(send_down, st == 0))
+        def _():
+            field_down(1, k).start()
+
+        @pl.when(jnp.logical_and(iface, st == count(up_iface)))
+        def _():
+            send_face(1, k, st)
+
+        es[k, st] = edges_of(fld[1, st + 1, k])
+        edge(k, 0, st).start()
+        edge(k, 1, st).start()
+
+    def far_step(k):
         send_ca(k).wait_recv()
-        for st in range(2):
-            fld[1, st + 1, k] = fld[1, st + 1, k] * cb[at(st, k)]
-
-        @pl.when(send_up)
-        def _():
-            field_up(1, k).start()
-
-        @pl.when(send_down)
-        def _():
-            field_down(1, k).start()
-
-        @pl.when(iface)
-        def _():
-            send_face(1, k, count(up_iface))
-
-        for st in range(2):
-            es[k, st] = edges_of(fld[1, st + 1, k])
-        edge(k, 0).start()
-        edge(k, 1).start()
+        weight_step(k, 1 - h)
 
     def result_step(k):
         down_c, up_c, center, lateral = coefs(k)
@@ -468,7 +467,8 @@
     @pl.loop(0, slots)
     def _(k):
         slope_step(k)
-        weight_step(k)
+        weight_step(k, h)
+        far_step(k)
 
     pl.loop(0, slots)(result_step)
 
@@ -488,8 +488,9 @@
     def _(k):
         send_out(k, mine(k), 0).wait_send()
         send_out(k, mine(k), 1).wait_send()
-        edge(k, 0).wait_send()
-        edge(k, 1).wait_send()
+        for side in range(2):
+            for st in range(2):
+                edge(k, side, st).wait_send()
         for f in range(2):
             @pl.when(send_up)
             def _():
@@ -546,7 +547,7 @@
                 pltpu.VMEM((n_span * pad, NL), BF16),
                 dma((4,)), dma((3,)), dma((3,)), dma((3,)), dma((3,)),
                 dma((2, 3, 2)), dma((2, 3, 2)), dma((2, 3)), dma((2, 3)),
-                dma((NC, 2)), dma((3, 2, 2)), dma((3, 2)), dma((3, 2)), dma((3, 2)), dma((3, 2)),
+                dma((NC, 2)), dma((3, 2, 2)), dma((3, 2, 2)), dma((3, 2, 2)), dma((3, 2)), dma((3, 2)),
                 pltpu.SemaphoreType.REGULAR, pltpu.SemaphoreType.REGULAR,
             ],
             compiler_params=pltpu.CompilerParams(

time: 35.7 us -> 35.9 us (level)
  the two profiles are of different devices: /device:TPU:225 before, /device:TPU:228 now
where the time goes in v4:
time: 35.9 us; the launch traced here: 35.8 us
  Pallas kernels  35 us (97%)
  local copies, waits for them, and re-layouts  0.78 us (2%)
    pallas_call x1, Pallas kernels, local(): pl.pallas_call(body, out_shape=jax.ShapeDtypeStruct((NC, NL, CP), F32), i...  35 us
    unnamed x1, local copies, waits for them, and re-layouts  0.78 us

profile of v4, /device:TPU:228, one launch (start us, length us, event | category | flops | bytes accessed | tf_op | source)
XLA Modules:
  0.0 35.8 jit_solution(7325283869553244910)
XLA Ops:
  0.0 35.0 %adjoint_step.1 = f32[5,192,128]{2,1,0:T(8,128)S(1)} custom-call(f32[5,192,128]{2,1,0:T(8,128)} %bitcast.9, f32[5,192,128]{2,1,0:T(8,128)} %bitcast.10, bf16[3,320,320]{2,1,0:T(8,128)(2,1)} %bitcast.8, s32[24,128]{1,0:T(8,128)} %bitcast.11), custom_call_target="tpu_custom_call" | custom-call | tf_op jit(solution)/shard_map/adjoint_step/pallas_call | solution.py:526
  35.0 0.8 %copy.7 = f32[5,192,1,128]{3,2,1,0:T(1,128)} copy(f32[5,192,1,128]{3,2,1,0:T(1,128)S(1)} %bitcast.7) | data formatting | bytes 983040
